TPU v7x, 512 devices: a whole 4x8x8 slice. The times are simulated.
512 devices in a mesh: row: 16 (over x, y_lo), col: 16 (over z, core), dp: 2 (over y_hi).
Axes of the slice: x: 4, y: 8 (y_hi: 2, y_lo: 4; y = y_hi * 4 + y_lo), z: 8, core: 2. Of those that a mesh axis runs over, the one named last changes fastest.
Arguments:
- grad_output: bfloat16 [2, 2048, 8192], P('dp', 'col', 'row'), may hold values from -0.09375 to 0.09375
- block_input: bfloat16 [2, 2048, 8192], P('dp', 'col', 'row'), may hold values from -6 to 6
- query_branch: bfloat16 [2, 2048, 8192], P('dp', 'row', 'col'), may hold values from -6 to 6
- key_branch: bfloat16 [2, 2048, 8192], P('dp', 'row', 'col'), may hold values from -6 to 6
- value_branch: bfloat16 [2, 2048, 8192], P('dp', 'row', 'col'), may hold values from -6 to 6
- out_weight: bfloat16 [8192, 8192], P('row', 'col'), may hold values from -0.0625 to 0.0625
- filters: float32 [512, 128], P('col'), may hold values from -0.5 to 0.5
Outputs:
- out_weight_grad: float32 [8192, 8192], P('row', 'col')
- value_weight_grad: float32 [8192, 8192], P('col', 'row')
- filter_grad: float32 [512, 128], P('col')
All inputs are finite; a program needn't handle non-finite values.
Results may differ from a plain program's by a relative error of at most 0.0029.
Values may be sent and summed in bfloat16 or wider, within the bound.
A program may use at most 128 MiB of HBM per device.

v0:
```python
import jax
import jax.numpy as jnp
from jax import lax
from jax.sharding import PartitionSpec as P

highest = lax.Precision.HIGHEST


def toeplitz(taps, tok_rows, causal):
    filter_len = taps.shape[1]
    out_pos = lax.broadcasted_iota(jnp.int32, (tok_rows, tok_rows + filter_len), 0)
    in_pos = lax.broadcasted_iota(jnp.int32, (tok_rows, tok_rows + filter_len), 1)
    lagged = out_pos + filter_len - in_pos if causal else in_pos - out_pos
    inside = (lagged >= 0) & (lagged < filter_len)
    picked = jnp.take(taps, jnp.clip(lagged, 0, filter_len - 1), axis=1)
    return jnp.where(inside[None], picked, 0.0)


def grouped_apply(table, signal, groups):
    blocks, extent, channels = signal.shape
    split = signal.reshape(blocks, extent, groups, channels // groups)
    result = jnp.einsum("gts,bsgc->btgc", table, split, precision=highest)
    return result.reshape(blocks, table.shape[1], channels)


def taps_partial(delta_mix, mixed_ext, groups, filter_len):
    blocks, tok_rows, channels = delta_mix.shape
    left_side = delta_mix.reshape(blocks, tok_rows, groups, channels // groups)
    right_side = mixed_ext.reshape(blocks, tok_rows + filter_len, groups, channels // groups)
    products = jnp.einsum("btgc,bsgc->gts", left_side, right_side, precision=highest)
    extent = tok_rows + filter_len
    flipped = products[:, :, ::-1]
    padded = jnp.pad(flipped, ((0, 0), (0, 0), (0, tok_rows)))
    flat_rows = padded.reshape(groups, -1)[:, : tok_rows * (extent + tok_rows - 1)]
    skewed = flat_rows.reshape(groups, tok_rows, extent + tok_rows - 1)
    column_sums = jnp.sum(skewed, axis=1)
    return column_sums[:, tok_rows - 1 : tok_rows - 1 + filter_len]


def local(grad_output, block_input, query_branch, key_branch, value_branch, out_weight, filters):
    filter_len = filters.shape[1]
    groups = filters.shape[0]
    tok_rows = query_branch.shape[1]
    channels = query_branch.shape[2]
    grads_all, inputs_all = (
        lax.all_gather(grad_output[0], "col", axis=0, tiled=True),
        lax.all_gather(block_input[0], "col", axis=0, tiled=True),
    )
    row_devices = lax.axis_size("row")
    sub_width = channels // row_devices
    delta_turned = lax.psum_scatter(
        lax.dot_general(
            out_weight, grads_all, (((0,), (1,)), ((), ())), preferred_element_type=jnp.float32
        ),
        "row",
        scatter_dimension=0,
        tiled=True,
    )
    queries, keys_here, values_here = (
        lax.all_to_all(query_branch[0], "row", split_axis=1, concat_axis=0, tiled=True),
        lax.all_to_all(key_branch[0], "row", split_axis=1, concat_axis=0, tiled=True),
        lax.all_to_all(value_branch[0], "row", split_axis=1, concat_axis=0, tiled=True),
    )
    delta_out = delta_turned.T
    local_groups = sub_width // (channels // groups)
    first_group = lax.axis_index("row") * local_groups
    my_taps = lax.dynamic_slice_in_dim(filters, first_group, local_groups, 0)
    mixed = keys_here.astype(jnp.float32) * values_here.astype(jnp.float32)
    mixed_blocks = mixed.reshape(row_devices, tok_rows, sub_width)
    earlier = jnp.concatenate(
        [
            jnp.zeros((1, filter_len, sub_width), jnp.float32),
            mixed_blocks[:-1, tok_rows - filter_len :],
        ],
        axis=0,
    )
    mixed_ext = jnp.concatenate([earlier, mixed_blocks], axis=1)
    conv_out = grouped_apply(toeplitz(my_taps, tok_rows, True), mixed_ext, local_groups).reshape(
        -1, sub_width
    )
    gated = (queries.astype(jnp.float32) * conv_out).astype(jnp.bfloat16)
    delta_mix = delta_out * queries.astype(jnp.float32)
    delta_blocks = delta_mix.reshape(row_devices, tok_rows, sub_width)
    later_part = jnp.concatenate(
        [delta_blocks[1:, :filter_len], jnp.zeros((1, filter_len, sub_width), jnp.float32)], axis=0
    )
    delta_ext = jnp.concatenate([delta_blocks, later_part], axis=1)
    delta_conv = grouped_apply(toeplitz(my_taps, tok_rows, False), delta_ext, local_groups).reshape(
        -1, sub_width
    )
    delta_value = (delta_conv * keys_here.astype(jnp.float32)).astype(jnp.bfloat16)
    my_terms = taps_partial(delta_blocks, mixed_ext, local_groups, filter_len)
    taps_local = lax.dynamic_update_slice_in_dim(
        jnp.zeros(filters.shape, jnp.float32), my_terms, first_group, 0
    )
    gated_all, value_all = (
        lax.all_gather(gated, "row", axis=1, tiled=True),
        lax.all_gather(delta_value, "row", axis=1, tiled=True),
    )
    out_grad = lax.dot_general(
        grads_all, gated_all, (((0,), (0,)), ((), ())), preferred_element_type=jnp.float32
    )
    value_grad = lax.dot_general(
        value_all, inputs_all, (((0,), (0,)), ((), ())), preferred_element_type=jnp.float32
    )
    out_grad, value_grad = lax.psum((out_grad, value_grad), "dp")
    taps_total = lax.psum(taps_local, ("row", "dp"))
    return (out_grad, value_grad, taps_total)


def solution(mesh):
    in_specs = (
        P("dp", "col", "row"),
        P("dp", "col", "row"),
        P("dp", "row", "col"),
        P("dp", "row", "col"),
        P("dp", "row", "col"),
        P("row", "col"),
        P("col", None),
    )
    out_specs = (P("row", "col"), P("col", "row"), P("col", None))
    return jax.shard_map(local, mesh=mesh, in_specs=in_specs, out_specs=out_specs, check_vma=False)
```

profile of v0, /device:TPU:64, one launch (start us, length us, event | category | flops | bytes accessed | tf_op | source)
XLA Modules:
  0.0 689.4 jit_solution(379694975442089937)
XLA Ops:
  8.0 48.5 %all-gather.11.cloned.1.call-done = bf16[1,2048,512]{2,1,0:T(8,128)(2,1)} async-done(((bf16[1,128,512]{2,1,0:T(8,128)(2,1)}), bf16[1,2048,512]{2,1,0:T(8,128)(2,1)}) %all-gather.11.cloned.1.call-update) | async-done | bytes 2097168 | tf_op jit(solution)/shard_map/all_gather | solution.py:46
  56.5 4.8 fusion.2
  61.4 0.9 copy-done.2
  62.2 0.8 copy.40
  63.0 7.1 %all-to-all-start.2 = ((bf16[128,16,32]{0,2,1:T(8,128)(2,1)}), bf16[128,16,32]{0,2,1:T(8,128)(2,1)S(1)}, u32[]{:S(2)}, u32[]{:S(2)}) async-start(bf16[128,16,32]{0,2,1:T(8,128)(2,1)} %bitcast.4), calls=%async_computation.2 | async-start | bytes 262144 | tf_op jit(solution)/shard_map/all_to_all | solution.py:62
  71.1 0.8 copy.38
  71.9 109.0 %gather_fusion = f32[32768,2]{1,0:T(8,128)} fusion(f32[2,128]{0,1:T(8,128)S(1)} %copy.62, s32[32768]{0:T(1024)S(1)} %broadcast_clamp_fusion.1), kind=kCustom, calls=%fused_computation.clone | custom fusion | bytes 655360 | tf_op jit(solution)/shard_map/jit(_take)/gather | solution.py:15
  180.9 10.0 %copy.46 = f32[128,256,2]{1,0,2:T(8,128)S(1)} copy(f32[128,256,2]{2,1,0:T(8,128)} %bitcast.113) | data formatting | bytes 524288 | tf_op jit(solution)/shard_map/jit(_take)/gather | solution.py:15
  190.9 0.8 copy.36
  191.9 7.5 %all-to-all-start.1 = ((bf16[128,16,32]{0,2,1:T(8,128)(2,1)}), bf16[128,16,32]{0,2,1:T(8,128)(2,1)S(1)}, u32[]{:S(2)}, u32[]{:S(2)}) async-start(bf16[128,16,32]{0,2,1:T(8,128)(2,1)} %bitcast.2), calls=%async_computation.1 | async-start | bytes 262144 | tf_op jit(solution)/shard_map/all_to_all | solution.py:61
  199.4 8.4 %all-to-all-done.1 = bf16[128,16,32]{0,2,1:T(8,128)(2,1)S(1)} async-done(((bf16[128,16,32]{0,2,1:T(8,128)(2,1)}), bf16[128,16,32]{0,2,1:T(8,128)(2,1)S(1)}, u32[]{:S(2)}, u32[]{:S(2)}) %all-to-all-start.1) | async-done | bytes 131104 | tf_op jit(solution)/shard_map/all_to_all | solution.py:61
  207.8 3.5 all-to-all-start
  212.4 7.3 %all-to-all-done = bf16[128,16,32]{0,2,1:T(8,128)(2,1)S(1)} async-done(((bf16[128,16,32]{0,2,1:T(8,128)(2,1)}), bf16[128,16,32]{0,2,1:T(8,128)(2,1)S(1)}, u32[]{:S(2)}, u32[]{:S(2)}) %all-to-all-start) | async-done | bytes 131104 | tf_op jit(solution)/shard_map/all_to_all | solution.py:60
  219.6 1.7 bitcast_multiply_fusion.2
  222.2 109.0 %gather_fusion.1 = f32[32768,2]{1,0:T(8,128)} fusion(f32[2,128]{0,1:T(8,128)S(1)} %copy.62, s32[32768]{0:T(1024)S(1)} %broadcast_clamp_fusion), kind=kCustom, calls=%fused_computation.1.clone | custom fusion | bytes 655360 | tf_op jit(solution)/shard_map/jit(_take)/gather | solution.py:15
  331.2 10.1 %copy.51 = f32[128,256,2]{1,0,2:T(8,128)S(1)} copy(f32[128,256,2]{2,1,0:T(8,128)} %bitcast.112) | data formatting | bytes 524288 | tf_op jit(solution)/shard_map/jit(_take)/gather | solution.py:15
  343.2 4.5 fusion.6
  347.7 1.5 all-gather.13.cloned.1.call-done
  349.2 91.4 %all-gather.9.cloned.1.call-done = bf16[2048,512]{0,1:T(8,128)(2,1)} async-done(((bf16[2048,32]{0,1:T(8,128)(2,1)}), bf16[2048,512]{0,1:T(8,128)(2,1)}) %all-gather.9.cloned.1.call-update) | async-done | bytes 2097168 | tf_op jit(solution)/shard_map/all_gather | solution.py:98
  440.6 4.4 fusion
  445.1 0.8 convolution_bitcast_fusion
  447.4 231.5 %psum.23 = f32[32,128]{1,0:T(8,128)} all-reduce(f32[32,128]{1,0:T(8,128)S(1)} %slice_dynamic-update-slice_fusion), channel_id=1, replica_groups=mesh['row'=16,'col'=16,'dp'=2] {'row','dp'}, use_global_device_ids=true, to_apply=%region_4.6 | all-reduce | flops 4096 | bytes 32768 | tf_op jit(solution)/shard_map/psum | solution.py:107
  678.9 2.6 copy.54
  681.5 1.0 copy.88
  (63 shorter events, 7.1 us)
Async XLA Ops:
  7.2 49.3 %copy-start = (bf16[512,512]{1,0:T(8,128)(2,1)S(1)}, bf16[512,512]{1,0:T(8,128)(2,1)}, u32[]{:S(2)}) copy-start(bf16[512,512]{1,0:T(8,128)(2,1)} %param.14) | copy-start | bytes 1572868
  7.2 49.3 %all-gather.11.cloned.1.call-start = ((), (), s32[]{:S(2)}) async-start(), calls=%async_computation.7 | async-start | bytes 2228224 | tf_op jit(solution)/shard_map/all_gather | solution.py:46
  7.9 211.7 %reduce-scatter.2.cloned.1.call-start = ((), (), s32[]{:S(2)}) async-start(), calls=%async_computation.5 | async-start | bytes 4456448 | tf_op jit(solution)/shard_map/reduce_scatter | solution.py:51
  61.3 0.9 copy-start.2
  61.3 9.7 %copy-start.3 = (bf16[1,128,512]{2,1,0:T(8,128)(2,1)S(1)}, bf16[1,128,512]{2,1,0:T(8,128)(2,1)}, u32[]{:S(2)}) copy-start(bf16[1,128,512]{2,1,0:T(8,128)(2,1)} %param.12) | copy-start | bytes 393220
  63.0 128.9 %all-to-all-start.2 = ((bf16[128,16,32]{0,2,1:T(8,128)(2,1)}), bf16[128,16,32]{0,2,1:T(8,128)(2,1)S(1)}, u32[]{:S(2)}, u32[]{:S(2)}) async-start(bf16[128,16,32]{0,2,1:T(8,128)(2,1)} %bitcast.4), calls=%async_computation.2 | async-start | bytes 262144 | tf_op jit(solution)/shard_map/all_to_all | solution.py:62
  180.9 10.0 %copy-start.4 = (bf16[1,128,512]{2,1,0:T(8,128)(2,1)S(1)}, bf16[1,128,512]{2,1,0:T(8,128)(2,1)}, u32[]{:S(2)}) copy-start(bf16[1,128,512]{2,1,0:T(8,128)(2,1)} %param.11) | copy-start | bytes 393220
  191.9 15.9 %all-to-all-start.1 = ((bf16[128,16,32]{0,2,1:T(8,128)(2,1)}), bf16[128,16,32]{0,2,1:T(8,128)(2,1)S(1)}, u32[]{:S(2)}, u32[]{:S(2)}) async-start(bf16[128,16,32]{0,2,1:T(8,128)(2,1)} %bitcast.2), calls=%async_computation.1 | async-start | bytes 262144 | tf_op jit(solution)/shard_map/all_to_all | solution.py:61
  207.8 11.9 %all-to-all-start = ((bf16[128,16,32]{0,2,1:T(8,128)(2,1)}), bf16[128,16,32]{0,2,1:T(8,128)(2,1)S(1)}, u32[]{:S(2)}, u32[]{:S(2)}) async-start(bf16[128,16,32]{0,2,1:T(8,128)(2,1)} %bitcast), calls=%async_computation | async-start | bytes 262144 | tf_op jit(solution)/shard_map/all_to_all | solution.py:60
  211.3 131.9 %all-gather.7.cloned.1.call-start = ((), (), s32[]{:S(2)}) async-start(), calls=%async_computation.4 | async-start | bytes 2228224 | tf_op jit(solution)/shard_map/all_gather | solution.py:97
  221.4 127.9 %all-gather.13.cloned.1.call-start = ((), (), s32[]{:S(2)}) async-start(), calls=%async_computation.8 | async-start | bytes 2228224 | tf_op jit(solution)/shard_map/all_gather | solution.py:47
  222.0 218.7 %all-gather.9.cloned.1.call-start = ((), (), s32[]{:S(2)}) async-start(), calls=%async_computation.6 | async-start | bytes 2228224 | tf_op jit(solution)/shard_map/all_gather | solution.py:98
  343.2 335.8 %all-reduce.6.cloned.1.call-start = ((), (), s32[]{:S(2)}) async-start(), calls=%async_computation.9 | async-start | bytes 4194304 | tf_op jit(solution)/shard_map/psum | solution.py:106
  678.9 2.6 copy-start.1
Sparse Core Ops, SparseCore 0:
  10.1 46.3 all-gather.10
  61.5 105.1 reduce-scatter.1
  221.5 84.2 all-gather.6
  307.8 41.4 all-gather.12
  351.7 88.8 all-gather.8
  445.2 122.4 all-reduce.5
where the time goes:
time: 690 us; the launch traced here: 689 us
  local copies, waits for them, and re-layouts  248 us (36%)
  blocking collectives  232 us (34%)
  waiting for transfers between devices  158 us (23%)
  starting transfers between devices  18.4 us (3%)
  matrix products  15.8 us (2%)
  between operations  14.4 us (2%)
    gather x4, local copies, waits for them, and re-layouts, toeplitz(): picked = jnp.take(taps, jnp.clip(lagged, 0, filter_len - 1), axis=1)  238 us
    psum x1, blocking collectives, local(): taps_total = lax.psum(taps_local, ('row', 'dp'))  232 us
    all_gather x1, waiting for transfers between devices, local(): lax.all_gather(delta_value, 'row', axis=1, tiled=True)  91.4 us
    all_gather x1, waiting for transfers between devices, local(): lax.all_gather(grad_output[0], 'col', axis=0, tiled=True)  48.5 us
  transfers between devices with their start and end apart: 9, of which 5 were waited for; matrix products, arithmetic and copies ran while one was open for 36% of the time, Pallas kernels for 0%

commit v1 on v0

--- a/solution.py
+++ b/solution.py
@@ -4,6 +4,11 @@
 from jax.sharding import PartitionSpec as P
 
 highest = lax.Precision.HIGHEST
+
+
+def one_after_other(array, axis_one, axis_two):
+    partial = lax.psum(array, axis_one)
+    return lax.psum(partial, axis_two)
 
 
 def toeplitz(taps, tok_rows, causal):
@@ -104,7 +109,7 @@
         value_all, inputs_all, (((0,), (0,)), ((), ())), preferred_element_type=jnp.float32
     )
     out_grad, value_grad = lax.psum((out_grad, value_grad), "dp")
-    taps_total = lax.psum(taps_local, ("row", "dp"))
+    taps_total = one_after_other(taps_local, "dp", "row")
     return (out_grad, value_grad, taps_total)
 
 

time: 690 us -> 588 us (0.85)
  the two profiles are of different devices: /device:TPU:64 before, /device:TPU:1 now
where the time goes in v1:
time: 588 us; the launch traced here: 587 us
  local copies, waits for them, and re-layouts  246 us (42%)
  waiting for transfers between devices  203 us (35%)
  blocking collectives  87.1 us (15%)
  starting transfers between devices  17.5 us (3%)
  matrix products  15.8 us (3%)
  between operations  14.4 us (2%)
    gather x4, local copies, waits for them, and re-layouts, toeplitz(): picked = jnp.take(taps, jnp.clip(lagged, 0, filter_len - 1), axis=1)  237 us
    all_gather x1, waiting for transfers between devices, local(): lax.all_gather(delta_value, 'row', axis=1, tiled=True)  81.3 us
    psum x1, blocking collectives, one_after_other(): return lax.psum(partial, axis_two)  75.4 us
    all_gather x1, waiting for transfers between devices, local(): lax.all_gather(grad_output[0], 'col', axis=0, tiled=True)  51.3 us
    psum x1, waiting for transfers between devices, local(): out_grad, value_grad = lax.psum((out_grad, value_grad), 'dp')  49.7 us
  transfers between devices with their start and end apart: 9, of which 6 were waited for; matrix products, arithmetic and copies ran while one was open for 43% of the time, Pallas kernels for 0%

profile of v1, /device:TPU:1, one launch (start us, length us, event | category | flops | bytes accessed | tf_op | source)
XLA Modules:
  0.0 587.0 jit_solution(16518102020407107777)
XLA Ops:
  8.0 51.3 %all-gather.11.cloned.1.call-done = bf16[1,2048,512]{2,1,0:T(8,128)(2,1)} async-done(((bf16[1,128,512]{2,1,0:T(8,128)(2,1)}), bf16[1,2048,512]{2,1,0:T(8,128)(2,1)}) %all-gather.11.cloned.1.call-update) | async-done | bytes 2097168 | tf_op jit(solution)/shard_map/all_gather | solution.py:51
  59.3 4.8 fusion.2
  64.1 0.9 copy-done.2
  65.8 6.8 %all-to-all-start.2 = ((bf16[128,16,32]{0,2,1:T(8,128)(2,1)}), bf16[128,16,32]{0,2,1:T(8,128)(2,1)S(1)}, u32[]{:S(2)}, u32[]{:S(2)}) async-start(bf16[128,16,32]{0,2,1:T(8,128)(2,1)} %bitcast.4), calls=%async_computation.2 | async-start | bytes 262144 | tf_op jit(solution)/shard_map/all_to_all | solution.py:67
  74.4 108.2 %gather_fusion = f32[32768,2]{1,0:T(8,128)} fusion(f32[2,128]{0,1:T(8,128)S(1)} %copy.62, s32[32768]{0:T(1024)S(1)} %broadcast_clamp_fusion.1), kind=kCustom, calls=%fused_computation.clone | custom fusion | bytes 655360 | tf_op jit(solution)/shard_map/jit(_take)/gather | solution.py:20
  182.7 10.0 %copy.46 = f32[128,256,2]{1,0,2:T(8,128)S(1)} copy(f32[128,256,2]{2,1,0:T(8,128)} %bitcast.113) | data formatting | bytes 524288 | tf_op jit(solution)/shard_map/jit(_take)/gather | solution.py:20
  192.6 0.8 copy.36
  193.6 7.0 %all-to-all-start.1 = ((bf16[128,16,32]{0,2,1:T(8,128)(2,1)}), bf16[128,16,32]{0,2,1:T(8,128)(2,1)S(1)}, u32[]{:S(2)}, u32[]{:S(2)}) async-start(bf16[128,16,32]{0,2,1:T(8,128)(2,1)} %bitcast.2), calls=%async_computation.1 | async-start | bytes 262144 | tf_op jit(solution)/shard_map/all_to_all | solution.py:66
  200.6 7.2 %all-to-all-done.1 = bf16[128,16,32]{0,2,1:T(8,128)(2,1)S(1)} async-done(((bf16[128,16,32]{0,2,1:T(8,128)(2,1)}), bf16[128,16,32]{0,2,1:T(8,128)(2,1)S(1)}, u32[]{:S(2)}, u32[]{:S(2)}) %all-to-all-start.1) | async-done | bytes 131104 | tf_op jit(solution)/shard_map/all_to_all | solution.py:66
  207.8 3.5 all-to-all-start
  212.4 6.1 %all-to-all-done = bf16[128,16,32]{0,2,1:T(8,128)(2,1)S(1)} async-done(((bf16[128,16,32]{0,2,1:T(8,128)(2,1)}), bf16[128,16,32]{0,2,1:T(8,128)(2,1)S(1)}, u32[]{:S(2)}, u32[]{:S(2)}) %all-to-all-start) | async-done | bytes 131104 | tf_op jit(solution)/shard_map/all_to_all | solution.py:65
  218.5 1.7 bitcast_multiply_fusion.2
  221.0 108.2 %gather_fusion.1 = f32[32768,2]{1,0:T(8,128)} fusion(f32[2,128]{0,1:T(8,128)S(1)} %copy.62, s32[32768]{0:T(1024)S(1)} %broadcast_clamp_fusion), kind=kCustom, calls=%fused_computation.1.clone | custom fusion | bytes 655360 | tf_op jit(solution)/shard_map/jit(_take)/gather | solution.py:20
  329.3 10.1 %copy.51 = f32[128,256,2]{1,0,2:T(8,128)S(1)} copy(f32[128,256,2]{2,1,0:T(8,128)} %bitcast.112) | data formatting | bytes 524288 | tf_op jit(solution)/shard_map/jit(_take)/gather | solution.py:20
  341.3 4.5 fusion.6
  345.8 5.9 all-gather.13.cloned.1.call-done
  351.7 81.3 %all-gather.9.cloned.1.call-done = bf16[2048,512]{0,1:T(8,128)(2,1)} async-done(((bf16[2048,32]{0,1:T(8,128)(2,1)}), bf16[2048,512]{0,1:T(8,128)(2,1)}) %all-gather.9.cloned.1.call-update) | async-done | bytes 2097168 | tf_op jit(solution)/shard_map/all_gather | solution.py:103
  432.9 4.4 fusion
  437.4 0.8 convolution_bitcast_fusion
  439.7 11.7 %psum.30 = f32[32,128]{1,0:T(8,128)S(1)} all-reduce(f32[32,128]{1,0:T(8,128)S(1)} %slice_dynamic-update-slice_fusion), channel_id=1, replica_groups=mesh['row'=16,'col'=16,'dp'=2] {'dp'}, use_global_device_ids=true, to_apply=%region_4.6 | all-reduce | flops 4096 | bytes 32768 | tf_op jit(solution)/shard_map/psum | solution.py:10
  451.4 75.4 %psum.31 = f32[32,128]{1,0:T(8,128)} all-reduce(f32[32,128]{1,0:T(8,128)S(1)} %psum.30), channel_id=1, replica_groups=mesh['row'=16,'col'=16,'dp'=2] {'row'}, use_global_device_ids=true, to_apply=%region_5.7 | all-reduce | flops 4096 | bytes 32768 | tf_op jit(solution)/shard_map/psum | solution.py:11
  526.8 49.7 %all-reduce.6.cloned.1.call-done = (f32[512,512]{0,1:T(8,128)}, f32[512,512]{1,0:T(8,128)}) async-done(((f32[512,512]{0,1:T(8,128)}, f32[512,512]{1,0:T(8,128)}), (f32[512,512]{0,1:T(8,128)}, f32[512,512]{1,0:T(8,128)})) %all-reduce.6.cloned.1.call-update) | async-done | bytes 2097168 | tf_op jit(solution)/shard_map/psum | solution.py:111
  576.5 2.6 copy.54
  579.2 1.0 copy.88
  (64 shorter events, 8.6 us)
Async XLA Ops:
  7.2 52.1 %copy-start = (bf16[512,512]{1,0:T(8,128)(2,1)S(1)}, bf16[512,512]{1,0:T(8,128)(2,1)}, u32[]{:S(2)}) copy-start(bf16[512,512]{1,0:T(8,128)(2,1)} %param.14) | copy-start | bytes 1572868
  7.2 52.1 %all-gather.11.cloned.1.call-start = ((), (), s32[]{:S(2)}) async-start(), calls=%async_computation.7 | async-start | bytes 2228224 | tf_op jit(solution)/shard_map/all_gather | solution.py:51
  7.9 210.6 %reduce-scatter.2.cloned.1.call-start = ((), (), s32[]{:S(2)}) async-start(), calls=%async_computation.5 | async-start | bytes 4456448 | tf_op jit(solution)/shard_map/reduce_scatter | solution.py:56
  64.1 0.9 copy-start.2
  64.1 9.4 %copy-start.3 = (bf16[1,128,512]{2,1,0:T(8,128)(2,1)S(1)}, bf16[1,128,512]{2,1,0:T(8,128)(2,1)}, u32[]{:S(2)}) copy-start(bf16[1,128,512]{2,1,0:T(8,128)(2,1)} %param.12) | copy-start | bytes 393220
  65.8 127.8 %all-to-all-start.2 = ((bf16[128,16,32]{0,2,1:T(8,128)(2,1)}), bf16[128,16,32]{0,2,1:T(8,128)(2,1)S(1)}, u32[]{:S(2)}, u32[]{:S(2)}) async-start(bf16[128,16,32]{0,2,1:T(8,128)(2,1)} %bitcast.4), calls=%async_computation.2 | async-start | bytes 262144 | tf_op jit(solution)/shard_map/all_to_all | solution.py:67
  182.6 10.0 %copy-start.4 = (bf16[1,128,512]{2,1,0:T(8,128)(2,1)S(1)}, bf16[1,128,512]{2,1,0:T(8,128)(2,1)}, u32[]{:S(2)}) copy-start(bf16[1,128,512]{2,1,0:T(8,128)(2,1)} %param.11) | copy-start | bytes 393220
  193.6 14.2 %all-to-all-start.1 = ((bf16[128,16,32]{0,2,1:T(8,128)(2,1)}), bf16[128,16,32]{0,2,1:T(8,128)(2,1)S(1)}, u32[]{:S(2)}, u32[]{:S(2)}) async-start(bf16[128,16,32]{0,2,1:T(8,128)(2,1)} %bitcast.2), calls=%async_computation.1 | async-start | bytes 262144 | tf_op jit(solution)/shard_map/all_to_all | solution.py:66
  207.8 10.7 %all-to-all-start = ((bf16[128,16,32]{0,2,1:T(8,128)(2,1)}), bf16[128,16,32]{0,2,1:T(8,128)(2,1)S(1)}, u32[]{:S(2)}, u32[]{:S(2)}) async-start(bf16[128,16,32]{0,2,1:T(8,128)(2,1)} %bitcast), calls=%async_computation | async-start | bytes 262144 | tf_op jit(solution)/shard_map/all_to_all | solution.py:65
  211.3 130.0 %all-gather.7.cloned.1.call-start = ((), (), s32[]{:S(2)}) async-start(), calls=%async_computation.4 | async-start | bytes 2228224 | tf_op jit(solution)/shard_map/all_gather | solution.py:102
  220.3 131.4 %all-gather.13.cloned.1.call-start = ((), (), s32[]{:S(2)}) async-start(), calls=%async_computation.8 | async-start | bytes 2228224 | tf_op jit(solution)/shard_map/all_gather | solution.py:52
  220.8 212.1 %all-gather.9.cloned.1.call-start = ((), (), s32[]{:S(2)}) async-start(), calls=%async_computation.6 | async-start | bytes 2228224 | tf_op jit(solution)/shard_map/all_gather | solution.py:103
  341.3 235.3 %all-reduce.6.cloned.1.call-start = ((), (), s32[]{:S(2)}) async-start(), calls=%async_computation.9 | async-start | bytes 4194304 | tf_op jit(solution)/shard_map/psum | solution.py:111
  576.5 2.6 copy-start.1
Sparse Core Ops, SparseCore 0:
  10.1 49.0 all-gather.10
  64.3 100.1 reduce-scatter.1
  220.4 77.4 all-gather.6
  299.9 51.7 all-gather.12
  354.2 78.7 all-gather.8
  437.5 138.9 all-reduce.5
